TPU v7x, 256 devices: a whole 4x4x8 slice. The times are simulated.
256 devices in a mesh: expert: 32 (over y, x, core), dp: 8 (over z).
Axes of the slice: x: 4, y: 4, z: 8, core: 2. Of those that a mesh axis runs over, the one named last changes fastest.
Arguments:
- tokens: bfloat16 [32768, 2048], P(('expert', 'dp')), may hold values from -6 to 6
- cotangent: bfloat16 [32768, 2048], P(('expert', 'dp')), may hold values from -6 to 6
- routes: int32 [32768, 4], P(('expert', 'dp')), may hold values from 0 to 31, all different within a row; in each aligned block of 128 rows (0 to 127, 128 to 255, ...) at most 24 rows name the same one
- gate_values: bfloat16 [32768, 4], P(('expert', 'dp')), may hold values from 0.099609375 to 1
- w_gate: bfloat16 [32, 2048, 512], P('expert', 'dp'), may hold values from -0.125 to 0.125
- w_up: bfloat16 [32, 2048, 512], P('expert', 'dp'), may hold values from -0.125 to 0.125
- w_down: bfloat16 [32, 512, 2048], P('expert', None, 'dp'), may hold values from -0.25 to 0.25
Outputs:
- token_grad: bfloat16 [32768, 2048], P(('expert', 'dp'))
- gate_weight_grad: bfloat16 [32, 2048, 512], P('expert', 'dp')
- up_weight_grad: bfloat16 [32, 2048, 512], P('expert', 'dp')
- down_weight_grad: bfloat16 [32, 512, 2048], P('expert', None, 'dp')
Inputs may be any that keep to these rules, and one draw needn't show every extreme that they name: `routes`: each row names 4 different experts. Among the rows of one device no expert is named more than 24 times, and some device names some expert exactly 24 times.
All inputs are finite; a program needn't handle non-finite values.
Results may differ from a plain program's by a relative error of at most 0.017.
Values may be sent and summed in bfloat16 or wider, within the bound.
No kernel may reach another device: no remote copies, remote signals or barrier semaphores. Data moves between devices by JAX's collectives and lax.ppermute only.
A program may use at most 128 MiB of HBM per device.

v0:
```python
import jax
import jax.numpy as jnp
from jax import lax
from jax.experimental.layout import Layout, with_layout_constraint
from jax.sharding import PartitionSpec as P


def slot_masks(routes, gate_values, experts, capacity):
    tok_dev = routes.shape[0]
    ids = jnp.arange(experts, dtype=jnp.int32)
    hit = routes[:, :, None] == ids[None, None, :]
    member = jnp.any(hit, axis=1)
    gate = jnp.sum(jnp.where(hit, gate_values.astype(jnp.float32)[:, :, None], 0.0), axis=1)
    row = lax.broadcasted_iota(jnp.int32, (tok_dev, tok_dev), 0)
    col = lax.broadcasted_iota(jnp.int32, (tok_dev, tok_dev), 1)
    earlier = (row < col).astype(jnp.bfloat16)
    before = lax.dot_general(
        member.astype(jnp.bfloat16),
        earlier,
        (((0,), (0,)), ((), ())),
        preferred_element_type=jnp.float32,
    ).astype(jnp.int32)
    rank = jnp.where(member.T, before, -1)
    place = rank[:, None, :] == jnp.arange(capacity, dtype=jnp.int32)[None, :, None]
    place = place.reshape(experts * capacity, tok_dev)
    weight = jnp.broadcast_to(gate.T[:, None, :], (experts, capacity, tok_dev)).reshape(
        experts * capacity, tok_dev
    )
    return (place.astype(jnp.bfloat16), jnp.where(place, weight, 0.0).astype(jnp.bfloat16))


def row_major(a):
    return with_layout_constraint(a, Layout(major_to_minor=(0, 1)))


def matmul(a, b, dims):
    return lax.dot_general(a, b, (dims, ((), ())), preferred_element_type=jnp.float32)


def local(tokens, cotangent, routes, gate_values, w_gate, w_up, w_down):
    experts = lax.axis_size("expert")
    tok_dev, model_width = tokens.shape
    fan_out = routes.shape[1]
    hidden_width = w_gate.shape[2]
    capacity = min(tok_dev, 3 * tok_dev * fan_out // (2 * experts))
    shard = jnp.concatenate([w_gate[0], w_up[0], w_down[0].T], axis=1)
    full = row_major(lax.all_gather(row_major(shard), "dp", axis=0, tiled=True))
    place, weighted = slot_masks(routes, gate_values, experts, capacity)

    def exchange(rows):
        return lax.all_to_all(
            rows.reshape(experts, capacity, model_width),
            "expert",
            split_axis=0,
            concat_axis=0,
            tiled=True,
        ).reshape(experts * capacity, model_width)

    x_rows = exchange(matmul(place, tokens, ((1,), (0,))).astype(jnp.bfloat16))
    scaled = exchange(matmul(weighted, cotangent, ((1,), (0,))).astype(jnp.bfloat16))
    pre = matmul(x_rows, full[:, : 2 * hidden_width], ((1,), (0,)))
    gate_pre = pre[:, :hidden_width]
    up_pre = pre[:, hidden_width:]
    sigmoid_gate = 1.0 / (1.0 + jnp.exp(-gate_pre))
    activated = gate_pre * sigmoid_gate
    hidden = (activated * up_pre).astype(jnp.bfloat16)
    hidden_grad = matmul(scaled, full[:, 2 * hidden_width :], ((1,), (0,)))
    gate_grad = (
        hidden_grad * up_pre * sigmoid_gate * (1.0 + gate_pre * (1.0 - sigmoid_gate))
    ).astype(jnp.bfloat16)
    up_grad = (hidden_grad * activated).astype(jnp.bfloat16)
    both_grad = jnp.concatenate([gate_grad, up_grad], axis=1)
    in_term = matmul(x_rows, both_grad, ((0,), (0,))).astype(jnp.bfloat16)
    down_term = matmul(scaled, hidden, ((0,), (0,))).astype(jnp.bfloat16)
    terms = jnp.concatenate([in_term, down_term], axis=1)
    sums = row_major(lax.psum_scatter(row_major(terms), "dp", scatter_dimension=0, tiled=True))
    row_grad = matmul(both_grad, full[:, : 2 * hidden_width], ((1,), (1,)))
    returned = exchange(row_grad.astype(jnp.bfloat16))
    token_grad = matmul(place, returned, ((0,), (0,))).astype(jnp.bfloat16)
    return (
        token_grad,
        sums[None, :, :hidden_width],
        sums[None, :, hidden_width : 2 * hidden_width],
        sums[:, 2 * hidden_width :].T[None],
    )


def solution(mesh):
    in_specs = (
        P(("expert", "dp"), None),
        P(("expert", "dp"), None),
        P(("expert", "dp"), None),
        P(("expert", "dp"), None),
        P("expert", "dp", None),
        P("expert", "dp", None),
        P("expert", None, "dp"),
    )
    out_specs = (
        P(("expert", "dp"), None),
        P("expert", "dp", None),
        P("expert", "dp", None),
        P("expert", None, "dp"),
    )
    return jax.shard_map(local, mesh=mesh, in_specs=in_specs, out_specs=out_specs, check_vma=False)
```

profile of v0, /device:TPU:1, one launch (start us, length us, event | category | flops | bytes accessed | tf_op | source)
XLA Modules:
  0.0 214.0 jit_solution(319687289944547735)
XLA Ops:
  7.2 1.1 copy.38
  8.4 2.0 pad_maximum_fusion.4
  10.5 0.7 fusion.15
  11.2 0.1 fusion.11
  11.3 0.2 bitcast_compare_fusion
  11.5 2.6 %convolution_convert_fusion.1 = bf16[768,2048]{1,0:T(8,128)(2,1)} fusion(pred[768,128]{1,0:T(32,128)(4,1)S(1)} %bitcast_compare_fusion, bf16[128,2048]{1,0:T(8,128)(2,1)S(1)} %copy-done), kind=kOutput, calls=%fused_computation.7 | convolution fusion | flops 404226048 | bytes 3768320 | tf_op jit(solution)/shard_map/dot_general | solution.py:37
  14.1 8.8 %all-to-all-start.1 = ((bf16[32,24,2048]{2,1,0:T(8,128)(2,1)}), bf16[32,24,2048]{2,1,0:T(8,128)(2,1)}, u32[]{:S(2)}, u32[]{:S(2)}) async-start(bf16[32,24,2048]{2,1,0:T(8,128)(2,1)} %bitcast.43), calls=%async_computation.1 | async-start | bytes 6291456 | tf_op jit(solution)/shard_map/all_to_all | solution.py:51
  23.0 0.2 fusion.12
  23.1 2.6 %convolution_convert_fusion.2 = bf16[768,2048]{1,0:T(8,128)(2,1)} fusion(bf16[768,128]{1,0:T(8,128)(2,1)S(1)} %fusion.12, bf16[128,2048]{1,0:T(8,128)(2,1)S(1)} %copy-done.1), kind=kOutput, calls=%fused_computation.8 | convolution fusion | flops 404226048 | bytes 3866624 | tf_op jit(solution)/shard_map/dot_general | solution.py:37
  25.7 36.4 %all-to-all-done.1 = bf16[32,24,2048]{2,1,0:T(8,128)(2,1)} async-done(((bf16[32,24,2048]{2,1,0:T(8,128)(2,1)}), bf16[32,24,2048]{2,1,0:T(8,128)(2,1)}, u32[]{:S(2)}, u32[]{:S(2)}) %all-to-all-start.1) | async-done | bytes 3145760 | tf_op jit(solution)/shard_map/all_to_all | solution.py:51
  62.1 7.3 %all-to-all-start = ((bf16[32,24,2048]{2,1,0:T(8,128)(2,1)}), bf16[32,24,2048]{2,1,0:T(8,128)(2,1)}, u32[]{:S(2)}, u32[]{:S(2)}) async-start(bf16[32,24,2048]{2,1,0:T(8,128)(2,1)} %bitcast.44), calls=%async_computation | async-start | bytes 6291456 | tf_op jit(solution)/shard_map/all_to_all | solution.py:51
  69.4 19.5 %all-gather.2.cloned.1.call-done = bf16[2048,1536]{1,0:T(8,128)(2,1)} async-done(((bf16[256,1536]{1,0:T(8,128)(2,1)}), bf16[2048,1536]{1,0:T(8,128)(2,1)}) %all-gather.2.cloned.1.call-update) | async-done | bytes 6291472 | tf_op jit(solution)/shard_map/all_gather | solution.py:47
  88.9 8.3 %fusion.2 = f32[768,1024]{0,1:T(8,128)} fusion(bf16[768,2048]{1,0:T(8,128)(2,1)} %bitcast.11, bf16[2048,1536]{1,0:T(8,128)(2,1)} %all-gather.2.cloned.1.call-done), kind=kOutput, calls=%fused_computation.4 | convolution fusion | flops 3221225472 | bytes 10485760 | tf_op jit(solution)/shard_map/dot_general | solution.py:37
  97.2 11.5 %all-to-all-done = bf16[32,24,2048]{2,1,0:T(8,128)(2,1)} async-done(((bf16[32,24,2048]{2,1,0:T(8,128)(2,1)}), bf16[32,24,2048]{2,1,0:T(8,128)(2,1)}, u32[]{:S(2)}, u32[]{:S(2)}) %all-to-all-start) | async-done | bytes 3145760 | tf_op jit(solution)/shard_map/all_to_all | solution.py:51
  108.7 4.9 %convolution_convert_fusion.3 = bf16[2048,512]{1,0:T(8,128)(2,1)S(1)} fusion(bf16[768,2048]{1,0:T(8,128)(2,1)} %bitcast.5, f32[768,1024]{0,1:T(8,128)} %fusion.2), kind=kOutput, calls=%fused_computation.9 | convolution fusion | flops 1614020608 | bytes 8388608 | tf_op jit(solution)/shard_map/dot_general | solution.py:37
  113.6 4.9 %multiply_convert_fusion.2 = (bf16[768,512]{0,1:T(8,128)(2,1)S(1)}, bf16[768,512]{0,1:T(8,128)(2,1)S(1)}) fusion(f32[768,1024]{0,1:T(8,128)S(1)} %copy-done.4, bf16[768,2048]{1,0:T(8,128)(2,1)} %bitcast.5, bf16[2048,1536]{1,0:T(8,128)(2,1)} %all-gather.2.cloned.1.call-done), kind=kOutput, calls=%fused_computation.17 | convolution fusion | flops 1615724544 | bytes 9961472 | tf_op jit(solution)/shard_map/dot_general | solution.py:37
  118.6 6.7 %convolution_convert_fusion = bf16[2048,1024]{1,0:T(8,128)(2,1)S(1)} fusion(bf16[768,2048]{1,0:T(8,128)(2,1)} %bitcast.11, bf16[768,512]{0,1:T(8,128)(2,1)S(1)} %get-tuple-element.21, bf16[768,512]{0,1:T(8,128)(2,1)S(1)} %get-tuple-element.20), kind=kOutput, calls=%fused_computation.1 | convolution fusion | flops 3226468352 | bytes 8912896 | tf_op jit(solution)/shard_map/dot_general | solution.py:37
  125.3 3.2 %pad_maximum_fusion = bf16[2048,1536]{1,0:T(8,128)(2,1)} fusion(bf16[2048,512]{1,0:T(8,128)(2,1)S(1)} %convolution_convert_fusion.3, bf16[2048,1024]{1,0:T(8,128)(2,1)S(1)} %convolution_convert_fusion), kind=kLoop, calls=%fused_computation | loop fusion | flops 12582912 | bytes 12582912 | tf_op jit(solution)/shard_map/concatenate | solution.py:75
  128.5 6.0 %fusion.4 = bf16[768,2048]{1,0:T(8,128)(2,1)S(1)} fusion(bf16[2048,1536]{1,0:T(8,128)(2,1)} %all-gather.2.cloned.1.call-done, bf16[768,512]{0,1:T(8,128)(2,1)S(1)} %get-tuple-element.21, bf16[768,512]{0,1:T(8,128)(2,1)S(1)} %get-tuple-element.20), kind=kOutput, calls=%fused_computation.6 | convolution fusion | flops 3225944064 | bytes 8912896 | tf_op jit(solution)/shard_map/dot_general | solution.py:37
  134.5 45.3 %all_to_all.15 = bf16[32,24,2048]{2,1,0:T(8,128)(2,1)S(1)} all-to-all(bf16[32,24,2048]{2,1,0:T(8,128)(2,1)S(1)} %bitcast.45), channel_id=1, replica_groups=mesh['expert'=32,'dp'=8] {'expert'}, dimensions={0} | all-to-all | bytes 6291456 | tf_op jit(solution)/shard_map/all_to_all | solution.py:51
  179.8 1.4 fusion.7
  181.2 23.1 %reduce-scatter.2.cloned.1.call-done = bf16[256,1536]{1,0:T(8,128)(2,1)} async-done(((bf16[2048,1536]{1,0:T(8,128)(2,1)}), bf16[256,1536]{1,0:T(8,128)(2,1)}) %reduce-scatter.2.cloned.1.call-update) | async-done | bytes 786448 | tf_op jit(solution)/shard_map/reduce_scatter | solution.py:76
  204.3 2.0 slice_bitcast_fusion
  206.3 0.8 copy.43
  (18 shorter events, 0.2 us)
Async XLA Ops:
  7.2 4.3 %copy-start = (bf16[128,2048]{1,0:T(8,128)(2,1)S(1)}, bf16[128,2048]{1,0:T(8,128)(2,1)}, u32[]{:S(2)}) copy-start(bf16[128,2048]{1,0:T(8,128)(2,1)} %param.7) | copy-start | bytes 1572868
  7.2 81.7 %all-gather.2.cloned.1.call-start = ((), (), s32[]{:S(2)}) async-start(), calls=%async_computation.4 | async-start | bytes 7077888 | tf_op jit(solution)/shard_map/all_gather | solution.py:47
  14.1 8.8 %copy-start.3 = (bf16[128,4]{0,1:T(4,128)(2,1)S(1)}, bf16[128,4]{0,1:T(4,128)(2,1)}, u32[]{:S(2)}) copy-start(bf16[128,4]{0,1:T(4,128)(2,1)} %param.10) | copy-start | bytes 3076
  14.1 8.8 %copy-start.2 = (s32[128,4]{0,1:T(4,128)S(1)}, s32[128,4]{0,1:T(4,128)}, u32[]{:S(2)}) copy-start(s32[128,4]{0,1:T(4,128)} %param.9) | copy-start | bytes 6148
  14.1 9.0 %copy-start.1 = (bf16[128,2048]{1,0:T(8,128)(2,1)S(1)}, bf16[128,2048]{1,0:T(8,128)(2,1)}, u32[]{:S(2)}) copy-start(bf16[128,2048]{1,0:T(8,128)(2,1)} %param.8) | copy-start | bytes 1572868
  14.1 48.0 %all-to-all-start.1 = ((bf16[32,24,2048]{2,1,0:T(8,128)(2,1)}), bf16[32,24,2048]{2,1,0:T(8,128)(2,1)}, u32[]{:S(2)}, u32[]{:S(2)}) async-start(bf16[32,24,2048]{2,1,0:T(8,128)(2,1)} %bitcast.43), calls=%async_computation.1 | async-start | bytes 6291456 | tf_op jit(solution)/shard_map/all_to_all | solution.py:51
  62.1 46.6 %all-to-all-start = ((bf16[32,24,2048]{2,1,0:T(8,128)(2,1)}), bf16[32,24,2048]{2,1,0:T(8,128)(2,1)}, u32[]{:S(2)}, u32[]{:S(2)}) async-start(bf16[32,24,2048]{2,1,0:T(8,128)(2,1)} %bitcast.44), calls=%async_computation | async-start | bytes 6291456 | tf_op jit(solution)/shard_map/all_to_all | solution.py:51
  69.4 135.0 %reduce-scatter.2.cloned.1.call-start = ((), (), s32[]{:S(2)}) async-start(), calls=%async_computation.5 | async-start | bytes 7077888 | tf_op jit(solution)/shard_map/reduce_scatter | solution.py:76
  108.7 4.9 %copy-start.4 = (f32[768,1024]{0,1:T(8,128)S(1)}, f32[768,1024]{0,1:T(8,128)}, u32[]{:S(2)}) copy-start(f32[768,1024]{0,1:T(8,128)} %fusion.2) | copy-start | bytes 9437188
Sparse Core Ops, SparseCore 0:
  10.5 78.3 all-gather.1
  128.6 75.6 reduce-scatter.1
where the time goes:
time: 214 us
  waiting for transfers between devices  90.5 us (42%)
  blocking collectives  45.3 us (21%)
  matrix products  37.6 us (18%)
  starting transfers between devices  16.1 us (8%)
  between operations  14.2 us (7%)
  other arithmetic  6.23 us (3%)
  local copies, waits for them, and re-layouts  4.04 us (2%)
    all_to_all x2, waiting for transfers between devices, exchange(): lax.all_to_all(rows.reshape(experts, capacity, model_width), 'expert', sp...  47.9 us
    all_to_all x1, blocking collectives, exchange(): lax.all_to_all(rows.reshape(experts, capacity, model_width), 'expert', sp...  45.3 us
    dot_general x8, matrix products, matmul(): lax.dot_general(a, b, (dims, ((), ())), preferred_element_type=jnp.float32)  37.5 us
    reduce_scatter x1, waiting for transfers between devices, local(): lax.psum_scatter(row_major(terms), 'dp', scatter_dimension=0, tiled=True)  23.1 us
    all_gather x1, waiting for transfers between devices, local(): full = row_major(lax.all_gather(row_major(shard), 'dp', axis=0, tiled=True))  19.5 us
    all_to_all x2, starting transfers between devices, exchange(): lax.all_to_all(rows.reshape(experts, capacity, model_width), 'expert', sp...  16 us
  transfers between devices with their start and end apart: 4, of which 4 were waited for; matrix products, arithmetic and copies ran while one was open for 10% of the time, Pallas kernels for 0%

commit v1 on v0

--- a/solution.py
+++ b/solution.py
@@ -38,13 +38,22 @@
 
 
 def local(tokens, cotangent, routes, gate_values, w_gate, w_up, w_down):
+
+    def frames_derive(frame_in, mesh_ax):
+        by_rank = []
+        for _ in range(jax.lax.axis_size(mesh_ax)):
+            by_rank.append(frame_in)
+        top = jax.lax.all_to_all(jnp.stack(by_rank), concat_axis=0, split_axis=0, axis_name=mesh_ax)
+        long_array = jnp.concatenate(top, axis=0)
+        return long_array
+
     experts = lax.axis_size("expert")
     tok_dev, model_width = tokens.shape
     fan_out = routes.shape[1]
     hidden_width = w_gate.shape[2]
     capacity = min(tok_dev, 3 * tok_dev * fan_out // (2 * experts))
     shard = jnp.concatenate([w_gate[0], w_up[0], w_down[0].T], axis=1)
-    full = row_major(lax.all_gather(row_major(shard), "dp", axis=0, tiled=True))
+    full = row_major(frames_derive(row_major(shard), "dp"))
     place, weighted = slot_masks(routes, gate_values, experts, capacity)
 
     def exchange(rows):

time: 214 us -> 357 us (1.67)
  waiting for transfers between devices: 90.5 us -> 225 us
  starting transfers between devices: 16.1 us -> 23.6 us
    all_to_all x0 -> x1, waiting for transfers between devices: none -> 139 us  [frames_derive(): jax.lax.all_to_all(jnp.stack(by_rank), concat_axis=0, split_axis=0, axis_...]
    all_to_all x2, waiting for transfers between devices: 47.9 us -> 69.7 us  [exchange(): lax.all_to_all(rows.reshape(experts, capacity, model_width), 'expert', sp...]
    all_gather x1 -> x0, waiting for transfers between devices: 19.5 us -> none  [local(): full = row_major(lax.all_gather(row_major(shard), 'dp', axis=0, tiled=True))]
    all_to_all x0 -> x1, starting transfers between devices: none -> 8.32 us  [frames_derive(): jax.lax.all_to_all(jnp.stack(by_rank), concat_axis=0, split_axis=0, axis_...]
    reduce_scatter x1, waiting for transfers between devices: 23.1 us -> 16.5 us  [local(): lax.psum_scatter(row_major(terms), 'dp', scatter_dimension=0, tiled=True)]
  transfers between devices with their start and end apart: 4 -> 4, of which waited for: 4 -> 4; matrix products, arithmetic and copies ran while one was open for 10% -> 5% of each run, Pallas kernels for 0% -> 0%
where the time goes in v1:
time: 357 us; the launch traced here: 356 us
  waiting for transfers between devices  225 us (63%)
  blocking collectives  45.3 us (13%)
  matrix products  37.6 us (11%)
  starting transfers between devices  23.6 us (7%)
  between operations  14.2 us (4%)
  local copies, waits for them, and re-layouts  6.24 us (2%)
  other arithmetic  4.38 us (1%)
    all_to_all x1, waiting for transfers between devices, frames_derive(): jax.lax.all_to_all(jnp.stack(by_rank), concat_axis=0, split_axis=0, axis_...  139 us
    all_to_all x2, waiting for transfers between devices, exchange(): lax.all_to_all(rows.reshape(experts, capacity, model_width), 'expert', sp...  69.7 us
    all_to_all x1, blocking collectives, exchange(): lax.all_to_all(rows.reshape(experts, capacity, model_width), 'expert', sp...  45.3 us
    dot_general x8, matrix products, matmul(): lax.dot_general(a, b, (dims, ((), ())), preferred_element_type=jnp.float32)  37.4 us
    reduce_scatter x1, waiting for transfers between devices, local(): lax.psum_scatter(row_major(terms), 'dp', scatter_dimension=0, tiled=True)  16.5 us
    all_to_all x2, starting transfers between devices, exchange(): lax.all_to_all(rows.reshape(experts, capacity, model_width), 'expert', sp...  15.1 us
    all_to_all x1, starting transfers between devices, frames_derive(): jax.lax.all_to_all(jnp.stack(by_rank), concat_axis=0, split_axis=0, axis_...  8.32 us
  transfers between devices with their start and end apart: 4, of which 4 were waited for; matrix products, arithmetic and copies ran while one was open for 5% of the time, Pallas kernels for 0%

profile of v1, /device:TPU:1, one launch (start us, length us, event | category | flops | bytes accessed | tf_op | source)
XLA Modules:
  0.0 356.5 jit_solution(2450930485351874938)
XLA Ops:
  7.2 0.8 fusion.15
  8.2 0.2 bitcast_compare_fusion
  8.4 2.6 convolution_convert_fusion.1
  11.0 8.8 %all-to-all-start.2 = ((bf16[32,24,2048]{2,1,0:T(8,128)(2,1)}), bf16[32,24,2048]{2,1,0:T(8,128)(2,1)}, u32[]{:S(2)}, u32[]{:S(2)}) async-start(bf16[32,24,2048]{2,1,0:T(8,128)(2,1)} %bitcast.44), calls=%async_computation.2 | async-start | bytes 6291456 | tf_op jit(solution)/shard_map/all_to_all | solution.py:60
  20.0 39.0 %all-to-all-done.2 = bf16[32,24,2048]{2,1,0:T(8,128)(2,1)} async-done(((bf16[32,24,2048]{2,1,0:T(8,128)(2,1)}), bf16[32,24,2048]{2,1,0:T(8,128)(2,1)}, u32[]{:S(2)}, u32[]{:S(2)}) %all-to-all-start.2) | async-done | bytes 3145760 | tf_op jit(solution)/shard_map/all_to_all | solution.py:60
  59.0 3.2 stack.2
  62.2 8.3 %all-to-all-start.1 = ((bf16[8,256,1536]{2,1,0:T(8,128)(2,1)}), bf16[8,256,1536]{2,1,0:T(8,128)(2,1)}, u32[]{:S(2)}, u32[]{:S(2)}) async-start(bf16[8,256,1536]{2,1,0:T(8,128)(2,1)} %stack.2), calls=%async_computation.1 | async-start | bytes 12582912 | tf_op jit(solution)/shard_map/all_to_all | solution.py:46
  70.5 0.2 fusion.12
  70.7 2.6 convolution_convert_fusion.2
  73.3 139.0 %all-to-all-done.1 = bf16[8,256,1536]{2,1,0:T(8,128)(2,1)} async-done(((bf16[8,256,1536]{2,1,0:T(8,128)(2,1)}), bf16[8,256,1536]{2,1,0:T(8,128)(2,1)}, u32[]{:S(2)}, u32[]{:S(2)}) %all-to-all-start.1) | async-done | bytes 6291488 | tf_op jit(solution)/shard_map/all_to_all | solution.py:46
  212.3 6.3 %all-to-all-start = ((bf16[32,24,2048]{2,1,0:T(8,128)(2,1)}), bf16[32,24,2048]{2,1,0:T(8,128)(2,1)}, u32[]{:S(2)}, u32[]{:S(2)}) async-start(bf16[32,24,2048]{2,1,0:T(8,128)(2,1)} %bitcast.45), calls=%async_computation | async-start | bytes 6291456 | tf_op jit(solution)/shard_map/all_to_all | solution.py:60
  218.6 0.2 reduce-scatter.2.cloned.1.call-start
  218.8 8.3 %fusion.2 = f32[768,1024]{0,1:T(8,128)} fusion(bf16[768,2048]{1,0:T(8,128)(2,1)} %bitcast.12, bf16[2048,1536]{1,0:T(8,128)(2,1)} %bitcast.10), kind=kOutput, calls=%fused_computation.4 | convolution fusion | flops 3221225472 | bytes 10485760 | tf_op jit(solution)/shard_map/dot_general | solution.py:37
  227.1 30.7 %all-to-all-done = bf16[32,24,2048]{2,1,0:T(8,128)(2,1)} async-done(((bf16[32,24,2048]{2,1,0:T(8,128)(2,1)}), bf16[32,24,2048]{2,1,0:T(8,128)(2,1)}, u32[]{:S(2)}, u32[]{:S(2)}) %all-to-all-start) | async-done | bytes 3145760 | tf_op jit(solution)/shard_map/all_to_all | solution.py:60
  257.8 5.9 %multiply_convert_fusion.2 = (bf16[768,512]{0,1:T(8,128)(2,1)S(1)}, bf16[768,512]{0,1:T(8,128)(2,1)S(1)}) fusion(f32[768,1024]{0,1:T(8,128)} %fusion.2, bf16[768,2048]{1,0:T(8,128)(2,1)} %bitcast.5, bf16[2048,1536]{1,0:T(8,128)(2,1)} %bitcast.10), kind=kOutput, calls=%fused_computation.17 | convolution fusion | flops 1615724544 | bytes 9961472 | tf_op jit(solution)/shard_map/dot_general | solution.py:37
  263.7 3.9 %convolution_convert_fusion.3 = bf16[2048,512]{1,0:T(8,128)(2,1)S(1)} fusion(bf16[768,2048]{1,0:T(8,128)(2,1)} %bitcast.5, f32[768,1024]{0,1:T(8,128)S(1)} %copy-done.7), kind=kOutput, calls=%fused_computation.9 | convolution fusion | flops 1614020608 | bytes 8388608 | tf_op jit(solution)/shard_map/dot_general | solution.py:37
  267.6 6.7 %convolution_convert_fusion = bf16[2048,1024]{1,0:T(8,128)(2,1)S(1)} fusion(bf16[768,2048]{1,0:T(8,128)(2,1)} %bitcast.12, bf16[768,512]{0,1:T(8,128)(2,1)S(1)} %get-tuple-element.21, bf16[768,512]{0,1:T(8,128)(2,1)S(1)} %get-tuple-element.20), kind=kOutput, calls=%fused_computation.1 | convolution fusion | flops 3226468352 | bytes 8912896 | tf_op jit(solution)/shard_map/dot_general | solution.py:37
  274.3 3.2 pad_maximum_fusion
  277.6 6.0 %fusion.4 = bf16[768,2048]{1,0:T(8,128)(2,1)S(1)} fusion(bf16[2048,1536]{1,0:T(8,128)(2,1)} %bitcast.10, bf16[768,512]{0,1:T(8,128)(2,1)S(1)} %get-tuple-element.21, bf16[768,512]{0,1:T(8,128)(2,1)S(1)} %get-tuple-element.20), kind=kOutput, calls=%fused_computation.6 | convolution fusion | flops 3225944064 | bytes 8912896 | tf_op jit(solution)/shard_map/dot_general | solution.py:37
  283.6 45.3 %all_to_all.20 = bf16[32,24,2048]{2,1,0:T(8,128)(2,1)S(1)} all-to-all(bf16[32,24,2048]{2,1,0:T(8,128)(2,1)S(1)} %bitcast.46), channel_id=1, replica_groups=mesh['expert'=32,'dp'=8] {'expert'}, dimensions={0} | all-to-all | bytes 6291456 | tf_op jit(solution)/shard_map/all_to_all | solution.py:60
  328.8 1.4 fusion.7
  330.3 16.5 %reduce-scatter.2.cloned.1.call-done = bf16[256,1536]{1,0:T(8,128)(2,1)} async-done(((bf16[2048,1536]{1,0:T(8,128)(2,1)}), bf16[256,1536]{1,0:T(8,128)(2,1)}) %reduce-scatter.2.cloned.1.call-update) | async-done | bytes 786448 | tf_op jit(solution)/shard_map/reduce_scatter | solution.py:85
  346.8 2.0 slice_bitcast_fusion
  348.8 0.8 copy.43
  (24 shorter events, 0.5 us)
Async XLA Ops:
  7.2 1.2 copy-start
  11.0 8.8 %copy-start.2 = (bf16[1,512,256]{2,1,0:T(8,128)(2,1)S(1)}, bf16[1,512,256]{2,1,0:T(8,128)(2,1)}, u32[]{:S(2)}) copy-start(bf16[1,512,256]{2,1,0:T(8,128)(2,1)} %param.13) | copy-start | bytes 786436
  11.0 8.9 %copy-start.3 = (bf16[1,256,512]{2,1,0:T(8,128)(2,1)S(1)}, bf16[1,256,512]{2,1,0:T(8,128)(2,1)}, u32[]{:S(2)}) copy-start(bf16[1,256,512]{2,1,0:T(8,128)(2,1)} %param.12) | copy-start | bytes 786436
  11.0 8.9 %copy-start.4 = (bf16[1,256,512]{2,1,0:T(8,128)(2,1)S(1)}, bf16[1,256,512]{2,1,0:T(8,128)(2,1)}, u32[]{:S(2)}) copy-start(bf16[1,256,512]{2,1,0:T(8,128)(2,1)} %param.11) | copy-start | bytes 786436
  11.0 48.0 %all-to-all-start.2 = ((bf16[32,24,2048]{2,1,0:T(8,128)(2,1)}), bf16[32,24,2048]{2,1,0:T(8,128)(2,1)}, u32[]{:S(2)}, u32[]{:S(2)}) async-start(bf16[32,24,2048]{2,1,0:T(8,128)(2,1)} %bitcast.44), calls=%async_computation.2 | async-start | bytes 6291456 | tf_op jit(solution)/shard_map/all_to_all | solution.py:60
  62.1 8.3 %copy-start.6 = (bf16[128,4]{0,1:T(4,128)(2,1)S(1)}, bf16[128,4]{0,1:T(4,128)(2,1)}, u32[]{:S(2)}) copy-start(bf16[128,4]{0,1:T(4,128)(2,1)} %param.10) | copy-start | bytes 3076
  62.2 8.3 %copy-start.5 = (s32[128,4]{0,1:T(4,128)S(1)}, s32[128,4]{0,1:T(4,128)}, u32[]{:S(2)}) copy-start(s32[128,4]{0,1:T(4,128)} %param.9) | copy-start | bytes 6148
  62.2 8.5 %copy-start.1 = (bf16[128,2048]{1,0:T(8,128)(2,1)S(1)}, bf16[128,2048]{1,0:T(8,128)(2,1)}, u32[]{:S(2)}) copy-start(bf16[128,2048]{1,0:T(8,128)(2,1)} %param.8) | copy-start | bytes 1572868
  62.2 150.1 %all-to-all-start.1 = ((bf16[8,256,1536]{2,1,0:T(8,128)(2,1)}), bf16[8,256,1536]{2,1,0:T(8,128)(2,1)}, u32[]{:S(2)}, u32[]{:S(2)}) async-start(bf16[8,256,1536]{2,1,0:T(8,128)(2,1)} %stack.2), calls=%async_computation.1 | async-start | bytes 12582912 | tf_op jit(solution)/shard_map/all_to_all | solution.py:46
  212.3 45.5 %all-to-all-start = ((bf16[32,24,2048]{2,1,0:T(8,128)(2,1)}), bf16[32,24,2048]{2,1,0:T(8,128)(2,1)}, u32[]{:S(2)}, u32[]{:S(2)}) async-start(bf16[32,24,2048]{2,1,0:T(8,128)(2,1)} %bitcast.45), calls=%async_computation | async-start | bytes 6291456 | tf_op jit(solution)/shard_map/all_to_all | solution.py:60
  218.6 128.2 %reduce-scatter.2.cloned.1.call-start = ((), (), s32[]{:S(2)}) async-start(), calls=%async_computation.5 | async-start | bytes 7077888 | tf_op jit(solution)/shard_map/reduce_scatter | solution.py:85
  257.8 5.9 %copy-start.7 = (f32[768,1024]{0,1:T(8,128)S(1)}, f32[768,1024]{0,1:T(8,128)}, u32[]{:S(2)}) copy-start(f32[768,1024]{0,1:T(8,128)} %fusion.2) | copy-start | bytes 9437188
Sparse Core Ops, SparseCore 0:
  277.7 69.0 reduce-scatter.1
